TPU v7x, 32 devices: a whole 2x2x4 slice. The times are simulated.
32 devices in a mesh: grp: 2 (over y), ha: 4 (over z), wa: 2 (over x), ta: 2 (over core).
Axes of the slice: x: 2, y: 2, z: 4, core: 2. Of those that a mesh axis runs over, the one named last changes fastest.
Arguments:
- frames: bfloat16 [8, 96, 16, 256], P(('grp', 'ta'), None, 'ha', 'wa'), parts along dimension 0, may hold values from -14 to 14
- cache_in: bfloat16 [4, 96, 16, 256], P('grp', None, 'ha', 'wa'), parts along dimension 0, may hold values from -4 to 4
- cache_mid: bfloat16 [4, 96, 16, 256], P('grp', None, 'ha', 'wa'), parts along dimension 0, may hold values from -4 to 4
- gain_in: float32 [96], replicated, may hold values from 0.25 to 1.75
- gain_mid: float32 [96], replicated, may hold values from 0.25 to 1.75
- weight_in: bfloat16 [3, 3, 96, 288], replicated, may hold values from -0.125 to 0.125
- bias_in: float32 [96], replicated, may hold values from -3 to 3
- weight_mid: bfloat16 [3, 3, 96, 288], replicated, may hold values from -0.125 to 0.125
- bias_mid: float32 [96], replicated, may hold values from -3 to 3
- cotangent: bfloat16 [8, 96, 16, 256], P(('grp', 'ta'), None, 'ha', 'wa'), parts along dimension 0, may hold values from -6 to 6
Outputs:
- decoded: bfloat16 [8, 96, 16, 256], P(('grp', 'ta'), None, 'ha', 'wa'), parts along dimension 0
- input_grad: float32 [8, 96, 16, 256], P(('grp', 'ta'), None, 'ha', 'wa'), parts along dimension 0
There are 2 independent parts, one for each index of `grp`. A program takes and returns all parts, laid end to end along the dimension named above; an argument that names none is the same for every part. Nothing has to cross between parts.
All inputs are finite; a program needn't handle non-finite values.
Results may differ from a plain program's by a relative error of at most 0.006.
Values may be sent and summed in bfloat16 or wider, within the bound.
A program may use at most 64 MiB of HBM per device.

v0:
```python
import jax
import jax.numpy as jnp
from jax import lax
from jax.sharding import PartitionSpec as P

epsilon = 1e-06


def passed_along(value, axis, steps):
    count = lax.axis_size(axis)
    leading, last = (max(0, -steps), min(count, count - steps))
    return lax.ppermute(value, axis, [(source, source + steps) for source in range(leading, last)])


def extended_2(array, sides, width):
    for axis, dim in sides:
        peers, length = (lax.axis_size(axis), array.shape[dim])
        up = [(i, (i + 1) % peers) for i in range(peers - 1)]
        down = [(j, i) for i, j in up]
        last = lax.slice_in_dim(array, length - width, length, axis=dim)
        leading = lax.slice_in_dim(array, 0, width, axis=dim)
        before = lax.ppermute(last, axis, up)
        after = lax.ppermute(leading, axis, down)
        array = jnp.concatenate([before, array, after], axis=dim)
    return array


def activate(values, gain):
    values = values.astype(jnp.float32)
    mean_square = jnp.mean(values * values, axis=1, keepdims=True)
    scaled = values * lax.rsqrt(mean_square + epsilon) * gain[None, :, None, None]
    return jax.nn.silu(scaled)


def act_back(values, gain, upstream):
    values = values.astype(jnp.float32)
    mean_square = jnp.mean(values * values, axis=1, keepdims=True)
    inverse = lax.rsqrt(mean_square + epsilon)
    gains = gain[None, :, None, None]
    scaled = values * inverse * gains
    sigmoid_part = jax.nn.sigmoid(scaled)
    weighted = gains * upstream * sigmoid_part * (1.0 + scaled * (1.0 - sigmoid_part))
    return inverse * weighted - values * inverse**3 * jnp.mean(
        weighted * values, axis=1, keepdims=True
    )


def flipped(weight):
    channels = weight.shape[2]
    five = weight.reshape(3, 3, channels, 3, channels)[::-1, ::-1, :, ::-1, :]
    return jnp.transpose(five, (0, 1, 4, 3, 2)).reshape(3, 3, channels, 3 * channels)


def convolve(padded, weight):
    count_frames = padded.shape[0] - 2
    height = padded.shape[2] - 2
    width = padded.shape[3] - 2
    stacked = jnp.concatenate(
        [padded[time_tap : time_tap + count_frames] for time_tap in range(3)], 1
    )
    summed = jnp.zeros((count_frames, weight.shape[2], height, width), jnp.float32)
    for row_tap in range(3):
        for col_tap in range(3):
            summed = summed + jnp.einsum(
                "ok,fkhw->fohw",
                weight[row_tap, col_tap],
                stacked[:, :, row_tap : row_tap + height, col_tap : col_tap + width],
                preferred_element_type=jnp.float32,
            )
    return summed


def earlier(values):
    return passed_along(values, "ta", 1)


def following(values):
    return passed_along(values, "ta", -1)


def inside_window(height, width):
    rows = lax.axis_index("ha") * height + jnp.arange(-1, height + 1, dtype=jnp.int32)
    cols = lax.axis_index("wa") * width + jnp.arange(-1, width + 1, dtype=jnp.int32)
    row_ok = (rows >= 0) & (rows < height * lax.axis_size("ha"))
    col_ok = (cols >= 0) & (cols < width * lax.axis_size("wa"))
    return (row_ok[:, None] & col_ok[None, :])[None, None]


def per_device(
    frames,
    cache_in,
    cache_mid,
    gain_in,
    gain_mid,
    weight_in,
    bias_in,
    weight_mid,
    bias_mid,
    cotangent,
):
    at_start = lax.axis_index("ta") == 0
    count_frames = frames.shape[0]
    height = frames.shape[2]
    width = frames.shape[3]
    stacked_inputs = jnp.concatenate(
        [earlier(frames), frames, cache_in, cache_mid, cotangent, following(cotangent)], 0
    )
    extended = extended_2(stacked_inputs, (("ha", 2), ("wa", 3)), 2)
    raw_part = extended[: count_frames + 2]
    cache_in_wide = extended[count_frames + 2 : count_frames + 4]
    cache_mid_cycle = extended[count_frames + 4 : count_frames + 6, :, 1:-1, 1:-1]
    padded_grad = extended[count_frames + 6 :]
    activated = activate(raw_part, gain_in).astype(jnp.bfloat16)
    padded_in = jnp.concatenate(
        [jnp.where(at_start, cache_in_wide, activated[:2]), activated[2:]], 0
    )
    hidden_cycle = (convolve(padded_in, weight_in) + bias_in[None, :, None, None]).astype(
        jnp.bfloat16
    )
    window_mask = inside_window(height, width)
    zero_mid = jnp.zeros((), jnp.bfloat16)
    active_cycle = jnp.where(
        window_mask, activate(hidden_cycle, gain_mid).astype(jnp.bfloat16), zero_mid
    )
    arrived_cycle = earlier(active_cycle)
    padded_mid = jnp.concatenate(
        [jnp.where(at_start, cache_mid_cycle, arrived_cycle), active_cycle], 0
    )
    residual = convolve(padded_mid, weight_mid) + bias_mid[None, :, None, None]
    decoded = (frames.astype(jnp.float32) + residual).astype(jnp.bfloat16)
    back_cycle = convolve(padded_grad, flipped(weight_mid))
    d_cycle = jnp.where(
        window_mask, act_back(hidden_cycle, gain_mid, back_cycle).astype(jnp.bfloat16), zero_mid
    )
    padded_back = jnp.concatenate([d_cycle, following(d_cycle)], 0)
    back_in = convolve(padded_back, flipped(weight_in))
    input_grad = cotangent.astype(jnp.float32) + act_back(frames, gain_in, back_in)
    return (decoded, input_grad)


def solution(mesh):
    placed = (
        P(("grp", "ta"), None, "ha", "wa"),
        P("grp", None, "ha", "wa"),
        P("grp", None, "ha", "wa"),
        P(),
        P(),
        P(),
        P(),
        P(),
        P(),
        P(("grp", "ta"), None, "ha", "wa"),
    )
    return jax.shard_map(
        per_device,
        mesh=mesh,
        in_specs=placed,
        out_specs=(P(("grp", "ta"), None, "ha", "wa"), P(("grp", "ta"), None, "ha", "wa")),
        check_vma=False,
    )
```

profile of v0, /device:TPU:0, one launch (start us, length us, event | category | flops | bytes accessed | tf_op | source)
XLA Modules:
  0.0 84.8 jit_solution(828491135651383448)
XLA Ops:
  0.6 1.1 %copy.93 = bf16[2,96,4,128]{1,3,2,0:T(8,128)(2,1)S(1)} copy(bf16[2,96,4,128]{3,2,1,0:T(4,128)(2,1)} %param.10) | data formatting | bytes 393216 | tf_op args[0]
  1.7 2.4 %collective-permute-start = (bf16[2,96,4,128]{1,3,2,0:T(8,128)(2,1)S(1)}, bf16[2,96,4,128]{1,3,2,0:T(8,128)(2,1)S(1)}, u32[]{:S(2)}, u32[]{:S(2)}) collective-permute-start(bf16[2,96,4,128]{1,3,2,0:T(8,128)(2,1)S(1)} %copy.93), channel_id=1, source_target_pairs={{0,1},{2,3},{4,5},{6,7},{8,9},{10,11},{12,13},{14,15},{16,17},{18,... | collective-permute-start | bytes 589832 | tf_op jit(solution)/shard_map/ppermute | solution.py:12
  4.2 1.1 %copy.98 = bf16[2,96,4,128]{1,3,2,0:T(8,128)(2,1)S(1)} copy(bf16[2,96,4,128]{3,2,1,0:T(4,128)(2,1)} %param.19) | data formatting | bytes 393216 | tf_op args[9]
  5.3 1.3 %collective-permute-start.1 = (bf16[2,96,4,128]{1,3,2,0:T(8,128)(2,1)S(1)}, bf16[2,96,4,128]{1,3,2,0:T(8,128)(2,1)S(1)}, u32[]{:S(2)}, u32[]{:S(2)}) collective-permute-start(bf16[2,96,4,128]{1,3,2,0:T(8,128)(2,1)S(1)} %copy.98), channel_id=1, source_target_pairs={{1,0},{3,2},{5,4},{7,6},{9,8},{11,10},{13,12},{15,14},{17,16},{19,... | collective-permute-start | bytes 589832 | tf_op jit(solution)/shard_map/ppermute | solution.py:12
  6.6 1.1 %copy.96 = bf16[2,96,4,128]{1,3,2,0:T(8,128)(2,1)S(1)} copy(bf16[2,96,4,128]{3,2,1,0:T(4,128)(2,1)} %param.11) | data formatting | bytes 393216 | tf_op args[1]
  7.7 1.1 %copy.97 = bf16[2,96,4,128]{1,3,2,0:T(8,128)(2,1)S(1)} copy(bf16[2,96,4,128]{3,2,1,0:T(4,128)(2,1)} %param.12) | data formatting | bytes 393216 | tf_op args[2]
  9.2 1.1 %copy.99 = bf16[12,96,2,128]{3,1,2,0:T(8,128)(2,1)} copy(bf16[12,96,2,128]{1,3,2,0:T(8,128)(2,1)S(1)} %get-tuple-element.10) | data formatting | bytes 1179648 | tf_op jit(solution)/shard_map/slice | solution.py:20
  10.3 5.2 %collective-permute-start.2 = (bf16[12,96,2,128]{3,1,2,0:T(8,128)(2,1)}, bf16[12,96,2,128]{3,1,2,0:T(8,128)(2,1)}, u32[]{:S(2)}, u32[]{:S(2)}) collective-permute-start(bf16[12,96,2,128]{3,1,2,0:T(8,128)(2,1)} %copy.99), channel_id=1, source_target_pairs={{0,4},{4,8},{8,12},{1,5},{5,9},{9,13},{2,6},{6,10},{10,14},{3,7},{... | collective-permute-start | bytes 1769480 | tf_op jit(solution)/shard_map/ppermute | solution.py:22
  15.5 1.1 %copy.100 = bf16[12,96,2,128]{3,1,2,0:T(8,128)(2,1)} copy(bf16[12,96,2,128]{1,3,2,0:T(8,128)(2,1)S(1)} %get-tuple-element.11) | data formatting | bytes 1179648 | tf_op jit(solution)/shard_map/slice | solution.py:21
  16.6 1.3 %collective-permute-start.3 = (bf16[12,96,2,128]{3,1,2,0:T(8,128)(2,1)}, bf16[12,96,2,128]{3,1,2,0:T(8,128)(2,1)}, u32[]{:S(2)}, u32[]{:S(2)}) collective-permute-start(bf16[12,96,2,128]{3,1,2,0:T(8,128)(2,1)} %copy.100), channel_id=1, source_target_pairs={{4,0},{8,4},{12,8},{5,1},{9,5},{13,9},{6,2},{10,6},{14,10},{7,3},{... | collective-permute-start | bytes 1769480 | tf_op jit(solution)/shard_map/ppermute | solution.py:23
  17.9 1.4 %copy.113 = bf16[3,3,96,288]{2,3,1,0:T(8,128)(2,1)S(1)} copy(bf16[3,3,96,288]{3,2,1,0:T(8,128)(2,1)} %param.17) | data formatting | bytes 995328 | tf_op args[7]
  19.4 1.2 %copy.124 = bf16[3,3,96,288]{2,3,1,0:T(8,128)(2,1)} copy(bf16[3,3,96,288]{3,2,1,0:T(8,128)(2,1)S(1)} %copy-done.2) | data formatting | bytes 995328 | tf_op args[5]
  20.5 0.9 %reverse_bitcast_fusion.1 = bf16[3,3,96,3,96]{4,2,3,1,0:T(8,128)(2,1)} fusion(bf16[3,3,96,3,96]{2,4,3,1,0:T(8,128)(2,1)S(1)} %bitcast.305), kind=kLoop, calls=%fused_computation.154 | loop fusion | bytes 995328 | tf_op jit(solution)/shard_map/transpose | solution.py:51
  21.5 7.0 %collective-permute-done.2 = bf16[12,96,2,128]{3,1,2,0:T(8,128)(2,1)} collective-permute-done((bf16[12,96,2,128]{3,1,2,0:T(8,128)(2,1)}, bf16[12,96,2,128]{3,1,2,0:T(8,128)(2,1)}, u32[]{:S(2)}, u32[]{:S(2)}) %collective-permute-start.2) | collective-permute-done | bytes 589856 | tf_op jit(solution)/shard_map/ppermute | solution.py:22
  28.6 1.4 %copy.101 = bf16[12,96,2,128]{1,3,2,0:T(8,128)(2,1)S(1)} copy(bf16[12,96,2,128]{3,1,2,0:T(8,128)(2,1)} %collective-permute-done.2) | data formatting | bytes 1179648 | tf_op jit(solution)/shard_map/ppermute | solution.py:22
  30.0 4.9 %collective-permute-done.3 = bf16[12,96,2,128]{3,1,2,0:T(8,128)(2,1)} collective-permute-done((bf16[12,96,2,128]{3,1,2,0:T(8,128)(2,1)}, bf16[12,96,2,128]{3,1,2,0:T(8,128)(2,1)}, u32[]{:S(2)}, u32[]{:S(2)}) %collective-permute-start.3) | collective-permute-done | bytes 589856 | tf_op jit(solution)/shard_map/ppermute | solution.py:23
  34.9 1.4 %copy.102 = bf16[12,96,2,128]{1,3,2,0:T(8,128)(2,1)S(1)} copy(bf16[12,96,2,128]{3,1,2,0:T(8,128)(2,1)} %collective-permute-done.3) | data formatting | bytes 1179648 | tf_op jit(solution)/shard_map/ppermute | solution.py:23
  36.5 3.5 %collective-permute-start.4 = (bf16[12,96,8,2]{1,3,2,0:T(2,128)(2,1)S(1)}, bf16[12,96,8,2]{1,3,2,0:T(2,128)(2,1)S(1)}, u32[]{:S(2)}, u32[]{:S(2)}) collective-permute-start(bf16[12,96,8,2]{1,3,2,0:T(2,128)(2,1)S(1)} %get-tuple-element.8), channel_id=1, source_target_pairs={{0,2},{1,3},{4,6},{5,7},{8,10},{9,11},{12,14},{13,15},{16,18},{17,... | collective-permute-start | bytes 110600 | tf_op jit(solution)/shard_map/ppermute | solution.py:22
  40.0 1.5 %collective-permute-start.5 = (bf16[12,96,8,2]{1,3,2,0:T(2,128)(2,1)S(1)}, bf16[12,96,8,2]{1,3,2,0:T(2,128)(2,1)S(1)}, u32[]{:S(2)}, u32[]{:S(2)}) collective-permute-start(bf16[12,96,8,2]{1,3,2,0:T(2,128)(2,1)S(1)} %get-tuple-element.9), channel_id=1, source_target_pairs={{2,0},{3,1},{6,4},{7,5},{10,8},{11,9},{14,12},{15,13},{18,16},{19,... | collective-permute-start | bytes 110600 | tf_op jit(solution)/shard_map/ppermute | solution.py:23
  41.5 0.9 %reverse_bitcast_fusion = bf16[3,3,96,3,96]{4,2,3,1,0:T(8,128)(2,1)} fusion(bf16[3,3,96,3,96]{2,4,3,1,0:T(8,128)(2,1)S(1)} %bitcast.304), kind=kLoop, calls=%fused_computation.153 | loop fusion | bytes 995328 | tf_op jit(solution)/shard_map/transpose | solution.py:51
  42.4 2.2 %copy.114 = bf16[3,3,96,3,96]{2,4,3,1,0:T(8,128)(2,1)} copy(bf16[3,3,96,3,96]{4,2,3,1,0:T(8,128)(2,1)} %reverse_bitcast_fusion.1) | data formatting | bytes 995328 | tf_op jit(solution)/shard_map/transpose | solution.py:51
  44.6 2.2 %copy.125 = bf16[3,3,96,3,96]{2,4,3,1,0:T(8,128)(2,1)} copy(bf16[3,3,96,3,96]{4,2,3,1,0:T(8,128)(2,1)} %reverse_bitcast_fusion) | data formatting | bytes 995328 | tf_op jit(solution)/shard_map/transpose | solution.py:51
  46.8 4.1 %fusion.8 = bf16[2,288,8,132]{1,3,2,0:T(8,128)(2,1)S(1)} fusion(bf16[12,96,8,2]{1,3,2,0:T(2,128)(2,1)S(1)} %collective-permute-done.5, bf16[12,96,8,2]{1,3,2,0:T(2,128)(2,1)S(1)} %collective-permute-done.4, bf16[12,96,2,128]{1,3,2,0:T(8,128)(2,1)S(1)} %copy.102, bf16[12,96,4,128]{1,3,2,0:T(8,128)(2,1)S(1)} %constant_dynamic-update-slice_fusion, ...), kind=kLoop, calls=%fused_computation.12 | loop fusion | flops 18247680 | bytes 3649536 | tf_op jit(solution)/shard_map/concatenate | solution.py:58
  55.7 1.7 %pad_maximum_fusion = bf16[12,96,8,132]{1,3,2,0:T(8,128)(2,1)S(1)} fusion(bf16[12,96,8,2]{1,3,2,0:T(2,128)(2,1)S(1)} %collective-permute-done.5, bf16[12,96,2,128]{1,3,2,0:T(8,128)(2,1)S(1)} %copy.102, bf16[12,96,4,128]{1,3,2,0:T(8,128)(2,1)S(1)} %constant_dynamic-update-slice_fusion, bf16[12,96,2,128]{1,3,2,0:T(8,128)(2,1)S(1)} %copy.101, ...), kind=kLoop, calls=%fused_computation | loop fusion | flops 12165120 | bytes 4866048 | tf_op jit(solution)/shard_map/concatenate | solution.py:24
  57.4 1.2 %fusion = f32[4,8,132]{2,1,0:T(8,128)S(1)} fusion(bf16[12,96,8,132]{1,3,2,0:T(8,128)(2,1)S(1)} %pad_maximum_fusion), kind=kLoop, calls=%fused_computation.3 | loop fusion | flops 1212288 | bytes 827904 | tf_op jit(solution)/shard_map/reduce_sum | solution.py:30
  58.6 1.1 %fusion.7 = bf16[4,96,8,132]{1,3,2,0:T(8,128)(2,1)S(1)} fusion(f32[96]{0:T(128)S(1)} %copy-done.9, f32[4,8,132]{2,1,0:T(8,128)S(1)} %add_rsqrt_fusion, bf16[12,96,8,132]{1,3,2,0:T(8,128)(2,1)S(1)} %pad_maximum_fusion), kind=kLoop, calls=%fused_computation.10 | loop fusion | flops 3244032 | bytes 1639296 | tf_op jit(solution)/shard_map/convert_element_type | solution.py:113
  60.0 0.8 fusion.11
  66.2 1.3 %multiply_reduce_fusion = (f32[2,6,130]{2,1,0:T(8,128)S(1)}, f32[2,96,6,130]{1,3,2,0:T(8,128)S(1)}) fusion(f32[2,96,6,130]{1,3,2,0:T(8,128)S(1)} %get-tuple-element.21, f32[96]{0:T(128)S(1)} %copy-done.8, f32[2,6,130]{2,1,0:T(8,128)S(1)} %get-tuple-element.17, f32[2,6,130,96]{3,2,1,0:T(8,128)S(1)} %fusion.29, f32[2,6,130,96]{3,2,1,0:T(8,128)S(1)} %fusion.31, ...), kind=kOutput, calls=%fused_computation.110 | convolution fusion | flops 89405160 | bytes 9470048 | tf_op jit(solution)/shard_map/ok,fkhw->fohw/dot_general | solution.py:64
  67.5 1.0 %fusion.114 = (bf16[2,96,6,130]{1,3,2,0:T(8,128)(2,1)S(1)}, bf16[2,96,6,130]{1,3,2,0:T(8,128)(2,1)S(1)}) fusion(f32[2,96,6,130]{1,3,2,0:T(8,128)S(1)} %get-tuple-element.21, f32[2,96,6,130]{1,3,2,0:T(8,128)S(1)} %get-tuple-element.23, f32[2,6,130]{2,1,0:T(8,128)S(1)} %broadcast_multiply_fusion, f32[2,6,130]{2,1,0:T(8,128)S(1)} %get-tuple-element.16, ...), kind=kLoop, calls=%fused_computation.156 | loop fusion | flops 2096640 | bytes 1817004 | tf_op jit(solution)/shard_map/jit(_where)/select_n | solution.py:132
  68.5 1.4 %collective-permute-start.7 = (bf16[2,96,6,130]{1,3,2,0:T(8,128)(2,1)S(1)}, bf16[2,96,6,130]{1,3,2,0:T(8,128)(2,1)S(1)}, u32[]{:S(2)}, u32[]{:S(2)}) collective-permute-start(bf16[2,96,6,130]{1,3,2,0:T(8,128)(2,1)S(1)} %get-tuple-element.14), channel_id=1, source_target_pairs={{1,0},{3,2},{5,4},{7,6},{9,8},{11,10},{13,12},{15,14},{17,16},{19,... | collective-permute-start | bytes 898568 | tf_op jit(solution)/shard_map/ppermute | solution.py:12
  70.0 3.3 %collective-permute-start.6 = (bf16[2,96,6,130]{1,3,2,0:T(8,128)(2,1)S(1)}, bf16[2,96,6,130]{1,3,2,0:T(8,128)(2,1)S(1)}, u32[]{:S(2)}, u32[]{:S(2)}) collective-permute-start(bf16[2,96,6,130]{1,3,2,0:T(8,128)(2,1)S(1)} %get-tuple-element.15), channel_id=1, source_target_pairs={{0,1},{2,3},{4,5},{6,7},{8,9},{10,11},{12,13},{14,15},{16,17},{18,... | collective-permute-start | bytes 898568 | tf_op jit(solution)/shard_map/ppermute | solution.py:12
  82.6 1.0 %copy.145 = f32[2,96,4,128]{3,2,1,0:T(4,128)} copy(f32[2,96,4,128]{3,1,2,0:T(8,128)S(1)} %fusion.126) | data formatting | bytes 786432
  (88 shorter events, 21.2 us)
Async XLA Ops:
  1.7 7.1 %collective-permute-start = (bf16[2,96,4,128]{1,3,2,0:T(8,128)(2,1)S(1)}, bf16[2,96,4,128]{1,3,2,0:T(8,128)(2,1)S(1)}, u32[]{:S(2)}, u32[]{:S(2)}) collective-permute-start(bf16[2,96,4,128]{1,3,2,0:T(8,128)(2,1)S(1)} %copy.93), channel_id=1, source_target_pairs={{0,1},{2,3},{4,5},{6,7},{8,9},{10,11},{12,13},{14,15},{16,17},{18,... | collective-permute-start | bytes 589832 | tf_op jit(solution)/shard_map/ppermute | solution.py:12
  5.3 3.7 %collective-permute-start.1 = (bf16[2,96,4,128]{1,3,2,0:T(8,128)(2,1)S(1)}, bf16[2,96,4,128]{1,3,2,0:T(8,128)(2,1)S(1)}, u32[]{:S(2)}, u32[]{:S(2)}) collective-permute-start(bf16[2,96,4,128]{1,3,2,0:T(8,128)(2,1)S(1)} %copy.98), channel_id=1, source_target_pairs={{1,0},{3,2},{5,4},{7,6},{9,8},{11,10},{13,12},{15,14},{17,16},{19,... | collective-permute-start | bytes 589832 | tf_op jit(solution)/shard_map/ppermute | solution.py:12
  10.3 9.1 %copy-start.2 = (bf16[3,3,96,288]{3,2,1,0:T(8,128)(2,1)S(1)}, bf16[3,3,96,288]{3,2,1,0:T(8,128)(2,1)}, u32[]{:S(2)}) copy-start(bf16[3,3,96,288]{3,2,1,0:T(8,128)(2,1)} %param.15) | copy-start | bytes 1492996
  10.3 18.3 %collective-permute-start.2 = (bf16[12,96,2,128]{3,1,2,0:T(8,128)(2,1)}, bf16[12,96,2,128]{3,1,2,0:T(8,128)(2,1)}, u32[]{:S(2)}, u32[]{:S(2)}) collective-permute-start(bf16[12,96,2,128]{3,1,2,0:T(8,128)(2,1)} %copy.99), channel_id=1, source_target_pairs={{0,4},{4,8},{8,12},{1,5},{5,9},{9,13},{2,6},{6,10},{10,14},{3,7},{... | collective-permute-start | bytes 1769480 | tf_op jit(solution)/shard_map/ppermute | solution.py:22
  16.6 18.3 %collective-permute-start.3 = (bf16[12,96,2,128]{3,1,2,0:T(8,128)(2,1)}, bf16[12,96,2,128]{3,1,2,0:T(8,128)(2,1)}, u32[]{:S(2)}, u32[]{:S(2)}) collective-permute-start(bf16[12,96,2,128]{3,1,2,0:T(8,128)(2,1)} %copy.100), channel_id=1, source_target_pairs={{4,0},{8,4},{12,8},{5,1},{9,5},{13,9},{6,2},{10,6},{14,10},{7,3},{... | collective-permute-start | bytes 1769480 | tf_op jit(solution)/shard_map/ppermute | solution.py:23
  36.3 5.1 %copy-start.1 = (bf16[3,3,96,288]{2,3,1,0:T(8,128)(2,1)S(1)}, bf16[3,3,96,288]{2,3,1,0:T(8,128)(2,1)}, u32[]{:S(2)}) copy-start(bf16[3,3,96,288]{2,3,1,0:T(8,128)(2,1)} %copy.124) | copy-start | bytes 1492996
  36.5 10.3 %collective-permute-start.4 = (bf16[12,96,8,2]{1,3,2,0:T(2,128)(2,1)S(1)}, bf16[12,96,8,2]{1,3,2,0:T(2,128)(2,1)S(1)}, u32[]{:S(2)}, u32[]{:S(2)}) collective-permute-start(bf16[12,96,8,2]{1,3,2,0:T(2,128)(2,1)S(1)} %get-tuple-element.8), channel_id=1, source_target_pairs={{0,2},{1,3},{4,6},{5,7},{8,10},{9,11},{12,14},{13,15},{16,18},{17,... | collective-permute-start | bytes 110600 | tf_op jit(solution)/shard_map/ppermute | solution.py:22
  40.0 6.8 %collective-permute-start.5 = (bf16[12,96,8,2]{1,3,2,0:T(2,128)(2,1)S(1)}, bf16[12,96,8,2]{1,3,2,0:T(2,128)(2,1)S(1)}, u32[]{:S(2)}, u32[]{:S(2)}) collective-permute-start(bf16[12,96,8,2]{1,3,2,0:T(2,128)(2,1)S(1)} %get-tuple-element.9), channel_id=1, source_target_pairs={{2,0},{3,1},{6,4},{7,5},{10,8},{11,9},{14,12},{15,13},{18,16},{19,... | collective-permute-start | bytes 110600 | tf_op jit(solution)/shard_map/ppermute | solution.py:23
  46.8 4.2 %copy-start.6 = (bf16[3,3,96,3,96]{2,4,3,1,0:T(8,128)(2,1)S(1)}, bf16[3,3,96,3,96]{2,4,3,1,0:T(8,128)(2,1)}, u32[]{:S(2)}) copy-start(bf16[3,3,96,3,96]{2,4,3,1,0:T(8,128)(2,1)} %copy.114) | copy-start | bytes 1492996
  55.7 2.9 %copy-start.9 = (f32[96]{0:T(128)S(1)}, f32[96]{0:T(128)}, u32[]{:S(2)}) copy-start(f32[96]{0:T(128)} %param.13) | copy-start | bytes 1156
  60.0 1.1 %copy-start.3 = (bf16[3,3,96,288]{3,2,1,0:T(8,128)(2,1)S(1)}, bf16[3,3,96,288]{3,2,1,0:T(8,128)(2,1)}, u32[]{:S(2)}) copy-start(bf16[3,3,96,288]{3,2,1,0:T(8,128)(2,1)} %param.15) | copy-start | bytes 1492996
  64.7 0.7 copy-start.11
  65.3 0.9 %copy-start.8 = (f32[96]{0:T(128)S(1)}, f32[96]{0:T(128)}, u32[]{:S(2)}) copy-start(f32[96]{0:T(128)} %param.14) | copy-start | bytes 1156
  67.5 2.5 %copy-start = (bf16[2,96,4,128]{3,2,1,0:T(4,128)(2,1)S(1)}, bf16[2,96,4,128]{3,2,1,0:T(4,128)(2,1)}, u32[]{:S(2)}) copy-start(bf16[2,96,4,128]{3,2,1,0:T(4,128)(2,1)} %param.10) | copy-start | bytes 589828
  68.5 5.5 %copy-start.5 = (bf16[3,3,96,3,96]{2,4,3,1,0:T(8,128)(2,1)S(1)}, bf16[3,3,96,3,96]{2,4,3,1,0:T(8,128)(2,1)}, u32[]{:S(2)}) copy-start(bf16[3,3,96,3,96]{2,4,3,1,0:T(8,128)(2,1)} %copy.125) | copy-start | bytes 1492996
  68.5 4.9 %collective-permute-start.7 = (bf16[2,96,6,130]{1,3,2,0:T(8,128)(2,1)S(1)}, bf16[2,96,6,130]{1,3,2,0:T(8,128)(2,1)S(1)}, u32[]{:S(2)}, u32[]{:S(2)}) collective-permute-start(bf16[2,96,6,130]{1,3,2,0:T(8,128)(2,1)S(1)} %get-tuple-element.14), channel_id=1, source_target_pairs={{1,0},{3,2},{5,4},{7,6},{9,8},{11,10},{13,12},{15,14},{17,16},{19,... | collective-permute-start | bytes 898568 | tf_op jit(solution)/shard_map/ppermute | solution.py:12
  70.0 7.1 %collective-permute-start.6 = (bf16[2,96,6,130]{1,3,2,0:T(8,128)(2,1)S(1)}, bf16[2,96,6,130]{1,3,2,0:T(8,128)(2,1)S(1)}, u32[]{:S(2)}, u32[]{:S(2)}) collective-permute-start(bf16[2,96,6,130]{1,3,2,0:T(8,128)(2,1)S(1)} %get-tuple-element.15), channel_id=1, source_target_pairs={{0,1},{2,3},{4,5},{6,7},{8,9},{10,11},{12,13},{14,15},{16,17},{18,... | collective-permute-start | bytes 898568 | tf_op jit(solution)/shard_map/ppermute | solution.py:12
  77.4 1.1 %copy-start.4 = (bf16[3,3,96,288]{3,2,1,0:T(8,128)(2,1)S(1)}, bf16[3,3,96,288]{3,2,1,0:T(8,128)(2,1)}, u32[]{:S(2)}) copy-start(bf16[3,3,96,288]{3,2,1,0:T(8,128)(2,1)} %param.17) | copy-start | bytes 1492996
  81.5 0.9 %copy-start.7 = (bf16[2,96,4,128]{3,2,1,0:T(4,128)(2,1)S(1)}, bf16[2,96,4,128]{3,2,1,0:T(4,128)(2,1)}, u32[]{:S(2)}) copy-start(bf16[2,96,4,128]{3,2,1,0:T(4,128)(2,1)} %param.19) | copy-start | bytes 589828
  82.2 1.3 %copy-start.10 = (f32[96]{0:T(128)S(1)}, f32[96]{0:T(128)}, u32[]{:S(2)}) copy-start(f32[96]{0:T(128)} %param.18) | copy-start | bytes 1156
where the time goes:
time: 85.5 us; the launch traced here: 84.8 us
  local copies, waits for them, and re-layouts  21.4 us (25%)
  starting transfers between devices  20 us (23%)
  matrix products  18.2 us (21%)
  other arithmetic  12.1 us (14%)
  waiting for transfers between devices  12 us (14%)
  between operations  1.17 us (1%)
    dot_general x36, matrix products, convolve(): jnp.einsum('ok,fkhw->fohw', weight[row_tap, col_tap], stacked[:, :, row_t...  18.2 us
    unnamed x37, local copies, waits for them, and re-layouts  10.1 us
    ppermute x2, starting transfers between devices, extended_2(): before = lax.ppermute(last, axis, up)  8.77 us
    ppermute x4, starting transfers between devices, passed_along(): lax.ppermute(value, axis, [(source, source + steps) for source in range(l...  8.47 us
    ppermute x2, waiting for transfers between devices, extended_2(): before = lax.ppermute(last, axis, up)  7.05 us
    concatenate x4, other arithmetic, convolve(): jnp.concatenate([padded[time_tap:time_tap + count_frames] for time_tap in...  6.25 us
    transpose x4, local copies, waits for them, and re-layouts, flipped(): jnp.transpose(five, (0, 1, 4, 3, 2)).reshape(3, 3, channels, 3 * channels)  6.16 us
    ppermute x2, waiting for transfers between devices, extended_2(): after = lax.ppermute(leading, axis, down)  4.9 us
  transfers between devices with their start and end apart: 8, of which 2 were waited for; matrix products, arithmetic and copies ran while one was open for 22% of the time, Pallas kernels for 0%

commit v1 on v0

v1 whole, which is shorter than its diff:
```python
import functools

import jax
import jax.numpy as jnp
from jax import lax
from jax.experimental import pallas as pl
from jax.experimental.pallas import tpu as pltpu
from jax.sharding import PartitionSpec as P

epsilon = 1e-06
BF, F32 = jnp.bfloat16, jnp.float32


def act(v, g):
    m = jnp.mean(v * v, axis=0, keepdims=True)
    z = v * lax.rsqrt(m + epsilon) * g
    return z * (1.0 / (1.0 + jnp.exp(-z)))


def act_back(v, g, d):
    m = jnp.mean(v * v, axis=0, keepdims=True)
    r = lax.rsqrt(m + epsilon)
    z = v * r * g
    s = 1.0 / (1.0 + jnp.exp(-z))
    q = g * d * s * (1.0 + z * (1.0 - s))
    return r * q - v * (r * r * r) * jnp.mean(q * v, axis=0, keepdims=True)


def kernel(
    n_ha, n_wa, x, w_in, w_mid, par, dec, grad,
    cb_in, cb_cot, cb_mid, cb_back, eb, e_out, stack, wts, acc, hid, send, recv,
):
    _, nf, nh, ch, nw = x.shape
    np_ = nh + 2
    ha, wa, ta = (lax.axis_index(a) for a in ("ha", "wa", "ta"))
    first, second = ta == 0, ta == 1
    lane = lax.broadcasted_iota(jnp.int32, (ch, nw), 1)
    half = nw // 2
    slot_row = lane % 8

    def have(dh, dw):
        ok = None
        for step, me, count in ((dh, ha, n_ha), (dw, wa, n_wa)):
            if step:
                this = (me > 0) if step < 0 else (me < count - 1)
                ok = this if ok is None else jnp.logical_and(ok, this)
        return ok

    def both(a, b):
        return b if a is None else a if b is None else jnp.logical_and(a, b)

    def when(cond, fn):
        if cond is None:
            fn()
        else:
            pl.when(cond)(fn)

    def target(dh, dw, dt):
        ids = {}
        if dh:
            ids["ha"] = ha + dh
        if dw:
            ids["wa"] = wa + dw
        if dt:
            ids["ta"] = 1 - ta
        return ids

    steps = [(dh, dw) for dh in (-1, 0, 1) for dw in (-1, 0, 1)]
    barrier = pltpu.get_barrier_semaphore()
    for dh, dw in steps:
        for dt in (0, 1):
            if dh or dw or dt:
                when(
                    have(dh, dw),
                    lambda dh=dh, dw=dw, dt=dt: pl.semaphore_signal(
                        barrier, inc=1, device_id=target(dh, dw, dt),
                        device_id_type=pl.DeviceIdType.MESH,
                    ),
                )
    rows_near = 1 + (ha > 0).astype(jnp.int32) + (ha < n_ha - 1).astype(jnp.int32)
    cols_near = 1 + (wa > 0).astype(jnp.int32) + (wa < n_wa - 1).astype(jnp.int32)

    used = [0]

    def transfer(src, dst, dh, dw, dt, sender=None, receiver=None):
        k = used[0]
        used[0] += 1
        copy = pltpu.make_async_remote_copy(
            src_ref=src, dst_ref=dst, send_sem=send.at[k], recv_sem=recv.at[k],
            device_id=target(dh, dw, dt), device_id_type=pl.DeviceIdType.MESH,
        )
        return copy, both(have(dh, dw), sender), both(have(-dh, -dw), receiver)

    def start(items):
        for copy, s, _ in items:
            when(s, copy.start)

    def arrive(items):
        for copy, _, r in items:
            when(r, copy.wait_recv)

    def leave(items):
        for copy, s, _ in items:
            when(s, copy.wait_send)

    def rows_of(top, bottom, cb, g, dt, sender=None, receiver=None):
        return [
            transfer(bottom, cb.at[g, :, 0], 1, 0, dt, sender, receiver),
            transfer(top, cb.at[g, :, nh + 1], -1, 0, dt, sender, receiver),
        ]

    def edges_of(stage, g, dt, sender=None, receiver=None):
        return [
            transfer(
                e_out.at[stage], eb.at[stage, g, 1 - dh, (dw + 1) // 2], dh, dw, dt,
                sender, receiver,
            )
            for dh, dw in steps if dw
        ]

    def make_edges(stage, tiles):
        e = jnp.zeros((ch, nw), F32)
        for (arr, f, h), tile in tiles:
            j = arr * 16 + f * 8 + h + 1
            e = jnp.where(lane == j, tile[:, :1], e)
            e = jnp.where(lane == half + j, tile[:, nw - 1 :], e)
        e_out[stage] = e.astype(BF)

    up, down, left, right = have(-1, 0), have(1, 0), have(0, -1), have(0, 1)

    def flag(cond):
        return jnp.full((ch, nw), cond.astype(jnp.int32), jnp.int32)

    side_ok = jnp.where(lane < half, flag(right), flag(left))
    row_ok = jnp.where(slot_row == 0, flag(up), jnp.where(slot_row == nh + 1, flag(down), 1))
    edge_ok = (side_ok * row_ok) > 0

    def merged(stage, g):
        v = [
            jnp.where(lane < half, eb[stage, g, s, 0].astype(F32), eb[stage, g, s, 1].astype(F32))
            for s in range(3)
        ]
        return jnp.where(
            slot_row == 0,
            pltpu.roll(v[0], nw - nh, 1),
            jnp.where(slot_row == nh + 1, pltpu.roll(v[2], nh, 1), v[1]),
        )

    first_tile, up_tile, down_tile = flag(first) > 0, flag(up) > 0, flag(down) > 0

    def put(conv, fp, hp, tile, edge, j):
        base = hp * 3 * ch
        if hp == 0:
            tile = jnp.where(up_tile, tile, 0.0)
        if hp == nh + 1:
            tile = jnp.where(down_tile, tile, 0.0)
        le = jnp.where(lane == 0, edge[:, half + j : half + j + 1], pltpu.roll(tile, 1, 1))
        ri = jnp.where(lane == nw - 1, edge[:, j : j + 1], pltpu.roll(tile, nw - 1, 1))
        stack[conv, fp, base : base + ch] = le.astype(BF)
        stack[conv, fp, base + ch : base + 2 * ch] = tile.astype(BF)
        stack[conv, fp, base + 2 * ch : base + 3 * ch] = ri.astype(BF)

    def convolve(conv, weight):
        for fp in range(nf + 2):
            taps = [t for t in range(3) if 0 <= fp - t < nf]
            lo, hi = taps[0] * ch, (taps[-1] + 1) * ch
            lhs = wts[weight, lo:hi]
            for h in range(0, nh, 2):
                a = stack[conv, fp, h * 3 * ch : (h + 3) * 3 * ch]
                b = stack[conv, fp, (h + 1) * 3 * ch : (h + 4) * 3 * ch]
                out = jnp.dot(
                    lhs, jnp.concatenate([a, b], axis=1), preferred_element_type=F32
                )
                for i, t in enumerate(taps):
                    f = fp - t
                    for k in range(2):
                        part = out[i * ch : (i + 1) * ch, k * nw : (k + 1) * nw]
                        if t == 0:
                            acc[f, h + k] = part
                        else:
                            acc[f, h + k] += part

    g_in, g_mid, b_in, b_mid = (par[:, i : i + 1] for i in range(4))

    own = [(f, h) for f in range(nf) for h in range(nh)]
    make_edges(0, [((a, f, h), x[a, f, h].astype(F32)) for a in range(4) for f, h in own])
    pl.semaphore_wait(barrier, 2 * rows_near * cols_near - 1)

    def x_rows(a, cb, g, dt, sender=None, receiver=None):
        return rows_of(x.at[a, :, 0], x.at[a, :, nh - 1], cb, g, dt, sender, receiver)

    e_own = edges_of(0, 0, 0)
    e_other = edges_of(0, 1, 1)
    s_cot = x_rows(3, cb_cot, 0, 0)
    s_cot += x_rows(3, cb_cot, 1, 1, second, first)
    s_cot += [transfer(x.at[3], cb_cot.at[1, :, 1 : nh + 1], 0, 0, 1, second, first)]
    s_in = x_rows(0, cb_in, 0, 0)
    s_in += x_rows(0, cb_in, 1, 1, first, second)
    s_in += [transfer(x.at[0], cb_in.at[1, :, 1 : nh + 1], 0, 0, 1, first, second)]
    s_in += x_rows(1, cb_in, 1, 0, first, first)
    s_cache = x_rows(2, cb_mid, 1, 0, first, first)
    stage0 = e_own + e_other + s_cot + s_in + s_cache
    start(stage0)

    for fwd, w in ((0, w_in), (1, w_mid)):
        for ab in range(9):
            block = w[ab].astype(F32)
            turned = w[8 - ab].astype(F32).T
            for t in range(3):
                wts[fwd, t * ch : (t + 1) * ch, ab * ch : (ab + 1) * ch] = block[
                    :, t * ch : (t + 1) * ch
                ].astype(BF)
                wts[2 + fwd, t * ch : (t + 1) * ch, ab * ch : (ab + 1) * ch] = turned[
                    (2 - t) * ch : (3 - t) * ch
                ].astype(BF)

    arrive(e_own + e_other + s_cot)
    raw_own, raw_other = merged(0, 0), merged(0, 1)
    e0 = jnp.where(edge_ok, raw_own, 0.0)
    e1 = jnp.where(edge_ok, jnp.where(first_tile, raw_other, 0.0), 0.0)
    for f in range(nf):
        for hp in range(np_):
            j = 3 * 16 + f * 8 + hp
            inner = 1 <= hp <= nh
            tile = x[3, f, hp - 1] if inner else cb_cot[0, f, hp]
            put(0, f, hp, tile.astype(F32), e0, j)
            tile = jnp.where(first_tile, cb_cot[1, f, hp].astype(F32), 0.0)
            put(0, nf + f, hp, tile, e1, j)
    convolve(0, 3)
    for f, h in own:
        grad[f, h] = acc[f, h]

    arrive(s_in)
    e_in0 = jnp.where(edge_ok, act(raw_own, g_in), 0.0)
    e_in1 = jnp.where(
        edge_ok,
        jnp.where(first_tile, pltpu.roll(raw_own, nw - 16, 1), act(raw_other, g_in)),
        0.0,
    )
    for f in range(nf):
        for hp in range(np_):
            j = f * 8 + hp
            inner = 1 <= hp <= nh
            tile = x[0, f, hp - 1] if inner else cb_in[0, f, hp]
            put(1, nf + f, hp, act(tile.astype(F32), g_in), e_in0, j)
            there = cb_in[1, f, hp].astype(F32)
            here = x[1, f, hp - 1].astype(F32) if inner else there
            put(1, f, hp, jnp.where(first_tile, here, act(there, g_in)), e_in1, j)
    convolve(1, 0)
    tiles = []
    for f, h in own:
        hidden = (acc[f, h] + b_in).astype(BF)
        hid[f, h] = hidden
        a = act(hidden.astype(F32), g_mid).astype(BF)
        cb_mid[0, f, h + 1] = a
        tiles.append(((0, f, h), a.astype(F32)))
    make_edges(1, tiles)

    def later(stage, cb, sender, receiver):
        top, bottom = cb.at[0, :, 1], cb.at[0, :, nh]
        items = edges_of(stage, 0, 0) + rows_of(top, bottom, cb, 0, 0)
        items += edges_of(stage, 1, 1, sender, receiver)
        items += rows_of(top, bottom, cb, 1, 1, sender, receiver)
        items += [
            transfer(
                cb.at[0, :, 1 : nh + 1], cb.at[1, :, 1 : nh + 1], 0, 0, 1, sender, receiver
            )
        ]
        return items

    stage1 = later(1, cb_mid, first, second)
    start(stage1)

    tiles = []
    for f, h in own:
        d = act_back(hid[f, h].astype(F32), g_mid, grad[f, h]).astype(BF)
        cb_back[0, f, h + 1] = d
        tiles.append(((0, f, h), d.astype(F32)))
    make_edges(2, tiles)
    stage2 = later(2, cb_back, second, first)
    start(stage2)

    arrive(s_cache)
    arrive(stage1)
    e0 = jnp.where(edge_ok, merged(1, 0), 0.0)
    e1 = jnp.where(
        edge_ok, jnp.where(first_tile, pltpu.roll(raw_own, nw - 32, 1), merged(1, 1)), 0.0
    )
    for f in range(nf):
        for hp in range(np_):
            j = f * 8 + hp
            inner = 1 <= hp <= nh
            put(2, nf + f, hp, cb_mid[0, f, hp].astype(F32), e0, j)
            there = cb_mid[1, f, hp].astype(F32)
            if inner:
                there = jnp.where(first_tile, x[2, f, hp - 1].astype(F32), there)
            put(2, f, hp, there, e1, j)
    convolve(2, 1)
    for f, h in own:
        dec[f, h] = (x[0, f, h].astype(F32) + acc[f, h] + b_mid).astype(BF)

    arrive(stage2)
    e0 = jnp.where(edge_ok, merged(2, 0), 0.0)
    e1 = jnp.where(edge_ok, jnp.where(first_tile, merged(2, 1), 0.0), 0.0)
    for f in range(nf):
        for hp in range(np_):
            j = f * 8 + hp
            put(3, f, hp, cb_back[0, f, hp].astype(F32), e0, j)
            tile = jnp.where(first_tile, cb_back[1, f, hp].astype(F32), 0.0)
            put(3, nf + f, hp, tile, e1, j)
    convolve(3, 2)
    for f, h in own:
        grad[f, h] = x[3, f, h].astype(F32) + act_back(x[0, f, h].astype(F32), g_in, acc[f, h])
    leave(stage0 + stage1 + stage2)


def per_device(
    frames, cache_in, cache_mid, gain_in, gain_mid, weight_in, bias_in, weight_mid,
    bias_mid, cotangent,
):
    nf, ch, nh, nw = frames.shape
    x = jnp.stack([frames, cache_in, cache_mid, cotangent]).transpose(0, 1, 3, 2, 4)
    par = jnp.stack([gain_in, gain_mid, bias_in, bias_mid], 1)
    k = 3 * ch
    vmem = pl.BlockSpec(memory_space=pltpu.VMEM)
    center = pltpu.VMEM((2, nf, nh + 2, ch, nw), BF)
    copies = 96
    dec, grad = pl.pallas_call(
        functools.partial(kernel, lax.axis_size("ha"), lax.axis_size("wa")),
        out_shape=(
            jax.ShapeDtypeStruct((nf, nh, ch, nw), BF),
            jax.ShapeDtypeStruct((nf, nh, ch, nw), F32),
        ),
        in_specs=[vmem] * 4,
        out_specs=(vmem, vmem),
        scratch_shapes=[
            center, center, center, center,
            pltpu.VMEM((3, 2, 3, 2, ch, nw), BF),
            pltpu.VMEM((3, ch, nw), BF),
            pltpu.VMEM((4, nf + 2, (nh + 2) * k, nw), BF),
            pltpu.VMEM((4, k, 9 * ch), BF),
            pltpu.VMEM((nf, nh, ch, nw), F32),
            pltpu.VMEM((nf, nh, ch, nw), BF),
            pltpu.SemaphoreType.DMA((copies,)),
            pltpu.SemaphoreType.DMA((copies,)),
        ],
        compiler_params=pltpu.CompilerParams(
            collective_id=0, has_side_effects=True, vmem_limit_bytes=60 << 20
        ),
    )(x, weight_in.reshape(9, ch, k), weight_mid.reshape(9, ch, k), par)
    return dec.transpose(0, 2, 1, 3), grad.transpose(0, 2, 1, 3)


def solution(mesh):
    moving = P(("grp", "ta"), None, "ha", "wa")
    cache = P("grp", None, "ha", "wa")
    placed = (moving, cache, cache, P(), P(), P(), P(), P(), P(), moving)
    return jax.shard_map(
        per_device, mesh=mesh, in_specs=placed, out_specs=(moving, moving), check_vma=False
    )
```

time: 85.5 us -> 33.2 us (0.39)
  Pallas kernels: 0 us -> 25.5 us
  starting transfers between devices: 20 us -> 0 us
  matrix products: 18.2 us -> 0 us
  local copies, waits for them, and re-layouts: 21.4 us -> 5.47 us
  waiting for transfers between devices: 12 us -> 0 us
  other arithmetic: 12.1 us -> 0.99 us
    pallas_call x0 -> x1, Pallas kernels: none -> 25.5 us  [per_device(): pl.pallas_call(functools.partial(kernel, lax.axis_size('ha'), lax.axis_si...]
    ppermute x8 -> x0, starting transfers between devices: 20 us -> none  [the longest x2 8.77 us: extended_2(): before = lax.ppermute(last, axis, up)]
    dot_general x36 -> x0, matrix products: 18.2 us -> none  [convolve(): jnp.einsum('ok,fkhw->fohw', weight[row_tap, col_tap], stacked[:, :, row_t...]
    ppermute x8 -> x0, waiting for transfers between devices: 12 us -> none  [the longest x2 7.05 us: extended_2(): before = lax.ppermute(last, axis, up)]
    concatenate x5 -> x0, other arithmetic: 7.94 us -> none  [the longest x4 6.25 us: convolve(): jnp.concatenate([padded[time_tap:time_tap + count_frames] for time_tap in...]
    unnamed x37 -> x16, local copies, waits for them, and re-layouts: 10.1 us -> 3.56 us
    transpose x4 -> x0, local copies, waits for them, and re-layouts: 6.16 us -> none  [flipped(): jnp.transpose(five, (0, 1, 4, 3, 2)).reshape(3, 3, channels, 3 * channels)]
    ppermute x2 -> x0, local copies, waits for them, and re-layouts: 2.88 us -> none  [the longest x1 1.44 us: extended_2(): after = lax.ppermute(leading, axis, down)]
  transfers between devices with their start and end apart: 8 -> 0, of which waited for: 2 -> 0; matrix products, arithmetic and copies ran while one was open for 22% -> 0% of each run, Pallas kernels for 0% -> 0%
where the time goes in v1:
time: 33.2 us; the launch traced here: 32.7 us
  Pallas kernels  25.5 us (77%)
  local copies, waits for them, and re-layouts  5.47 us (16%)
  other arithmetic  0.99 us (3%)
  between operations  0.7 us (2%)
    pallas_call x1, Pallas kernels, per_device(): pl.pallas_call(functools.partial(kernel, lax.axis_size('ha'), lax.axis_si...  25.5 us
    unnamed x16, local copies, waits for them, and re-layouts  3.56 us
    another operation x2, local copies, waits for them, and re-layouts, per_device(): jnp.stack([frames, cache_in, cache_mid, cotangent]).transpose(0, 1, 3, 2, 4)  1.19 us
    transpose x1, other arithmetic, per_device(): jnp.stack([frames, cache_in, cache_mid, cotangent]).transpose(0, 1, 3, 2, 4)  0.98 us
    another operation x1, local copies, waits for them, and re-layouts, per_device(): par = jnp.stack([gain_in, gain_mid, bias_in, bias_mid], 1)  0.73 us

profile of v1, /device:TPU:0, one launch (start us, length us, event | category | flops | bytes accessed | tf_op | source)
XLA Modules:
  0.0 32.7 jit_solution(1591621579111806557)
XLA Ops:
  0.6 0.0 copy-start.2
  0.6 0.0 copy-start.1
  0.7 1.1 %copy_bitcast_fusion = (bf16[1,2,96,4,128]{4,2,3,1,0:T(8,128)(2,1)S(1)}, bf16[1,2,96,4,128]{4,2,3,1,0:T(8,128)(2,1)S(1)}) fusion(bf16[2,96,4,128]{3,2,1,0:T(4,128)(2,1)} %param.19, bf16[2,96,4,128]{3,2,1,0:T(4,128)(2,1)} %param.12), kind=kLoop, calls=%fused_computation.1 | loop fusion | bytes 786432 | tf_op jit(solution)/shard_map/stack | solution.py:322
  1.8 0.0 copy-done.2
  1.8 0.0 copy-done.1
  1.8 0.1 copy_bitcast_fusion.2
  1.9 0.0 copy-start.6
  1.9 1.0 %maximum_bitcast_fusion.x = bf16[4,2,4,96,128]{4,3,2,1,0:T(8,128)(2,1)} fusion(bf16[1,2,96,4,128]{4,2,3,1,0:T(8,128)(2,1)S(1)} %get-tuple-element.10, bf16[1,2,96,4,128]{4,2,3,1,0:T(8,128)(2,1)S(1)} %get-tuple-element.11, bf16[1,2,96,4,128]{4,2,3,1,0:T(8,128)(2,1)S(1)} %get-tuple-element.12, bf16[1,2,96,4,128]{4,2,3,1,0:T(8,128)(2,1)S(1)} %get-tuple-element.13), kind=kLoop, calls=%fused_computation | loop fusion | flops 1179648 | bytes 1572864 | tf_op jit(solution)/shard_map/transpose | solution.py:322
  2.9 0.0 copy-start.3
  2.9 0.0 copy-start.4
  2.9 0.0 copy-start.5
  2.9 0.0 copy-done.6
  2.9 0.6 %copy-done.3 = f32[96]{0:T(128)S(1)} copy-done((f32[96]{0:T(128)S(1)}, f32[96]{0:T(128)}, u32[]{:S(2)}) %copy-start.3) | copy-done | bytes 408
  3.6 0.0 copy-done.4
  3.6 0.0 copy-done.5
  3.6 0.7 %copy.26.par = f32[96,4]{1,0:T(8,128)} copy(f32[96,4]{0,1:T(4,128)S(1)} %pad_maximum_fusion) | data formatting | bytes 3072 | tf_op jit(solution)/shard_map/stack | solution.py:323
  4.3 25.5 %shard_map.113 = (bf16[2,4,96,128]{3,2,1,0:T(8,128)(2,1)}, f32[2,4,96,128]{3,2,1,0:T(8,128)}) custom-call(bf16[4,2,4,96,128]{4,3,2,1,0:T(8,128)(2,1)} %maximum_bitcast_fusion.x, bf16[9,96,288]{2,1,0:T(8,128)(2,1)} %bitcast.18, bf16[9,96,288]{2,1,0:T(8,128)(2,1)} %bitcast.19, f32[96,4]{1,0:T(8,128)} %copy.26.par), custom_call_target="tpu_custom_call" | custom-call | tf_op jit(solution)/shard_map/pallas_call | solution.py:328
  29.9 0.0 copy-start
  29.9 2.0 %copy.28 = f32[2,96,4,128]{3,2,1,0:T(4,128)} copy(f32[2,96,4,128]{3,1,2,0:T(8,128)} %bitcast.20) | data formatting | bytes 786432
  31.9 0.0 copy-done
  31.9 0.8 %copy.27 = bf16[2,96,4,128]{3,2,1,0:T(4,128)(2,1)} copy(bf16[2,96,4,128]{3,1,2,0:T(8,128)(2,1)S(1)} %bitcast.21) | data formatting | bytes 393216
  (1 shorter events, 0.0 us)
Async XLA Ops:
  0.6 1.2 %copy-start.2 = (bf16[2,96,4,128]{3,2,1,0:T(4,128)(2,1)S(1)}, bf16[2,96,4,128]{3,2,1,0:T(4,128)(2,1)}, u32[]{:S(2)}) copy-start(bf16[2,96,4,128]{3,2,1,0:T(4,128)(2,1)} %param.10) | copy-start | bytes 589828
  0.6 1.2 %copy-start.1 = (bf16[2,96,4,128]{3,2,1,0:T(4,128)(2,1)S(1)}, bf16[2,96,4,128]{3,2,1,0:T(4,128)(2,1)}, u32[]{:S(2)}) copy-start(bf16[2,96,4,128]{3,2,1,0:T(4,128)(2,1)} %param.11) | copy-start | bytes 589828
  1.9 1.0 %copy-start.6 = (f32[96]{0:T(128)S(1)}, f32[96]{0:T(128)}, u32[]{:S(2)}) copy-start(f32[96]{0:T(128)} %param.13) | copy-start | bytes 1156
  2.9 0.7 %copy-start.3 = (f32[96]{0:T(128)S(1)}, f32[96]{0:T(128)}, u32[]{:S(2)}) copy-start(f32[96]{0:T(128)} %param.18) | copy-start | bytes 1156
  2.9 0.7 %copy-start.4 = (f32[96]{0:T(128)S(1)}, f32[96]{0:T(128)}, u32[]{:S(2)}) copy-start(f32[96]{0:T(128)} %param.16) | copy-start | bytes 1156
  2.9 0.7 %copy-start.5 = (f32[96]{0:T(128)S(1)}, f32[96]{0:T(128)}, u32[]{:S(2)}) copy-start(f32[96]{0:T(128)} %param.14) | copy-start | bytes 1156
  29.9 2.0 %copy-start = (bf16[2,4,96,128]{3,2,1,0:T(8,128)(2,1)S(1)}, bf16[2,4,96,128]{3,2,1,0:T(8,128)(2,1)}, u32[]{:S(2)}) copy-start(bf16[2,4,96,128]{3,2,1,0:T(8,128)(2,1)} %get-tuple-element.4) | copy-start | bytes 589828

commit v2 on v1

--- a/solution.py
+++ b/solution.py
@@ -27,15 +27,20 @@
 
 
 def kernel(
-    n_ha, n_wa, x, w_in, w_mid, par, dec, grad,
-    cb_in, cb_cot, cb_mid, cb_back, eb, e_out, stack, wts, acc, hid, send, recv,
+    n_ha, n_wa, x0, x1, x2, x3, w_in, w_mid, p0, p1, p2, p3, dec, grad,
+    cb_in, cb_cot, cb_mid, cb_back, eb0, eb, e_out0, e_out, stack, wts, acc, wide,
+    hid, send, recv,
 ):
-    _, nf, nh, ch, nw = x.shape
+    x = (x0, x1, x2, x3)
+    nf, nh, ch, nw = x0.shape
+    fold = 16
     np_ = nh + 2
     ha, wa, ta = (lax.axis_index(a) for a in ("ha", "wa", "ta"))
     first, second = ta == 0, ta == 1
     lane = lax.broadcasted_iota(jnp.int32, (ch, nw), 1)
     half = nw // 2
+    small_lane = lax.broadcasted_iota(jnp.int32, (fold, nw), 1)
+    small_row = small_lane % 8
     slot_row = lane % 8
 
     def have(dh, dw):
@@ -109,22 +114,31 @@
             transfer(top, cb.at[g, :, nh + 1], -1, 0, dt, sender, receiver),
         ]
 
-    def edges_of(stage, g, dt, sender=None, receiver=None):
+    def edges_of(source, landing, dt, sender=None, receiver=None):
         return [
             transfer(
-                e_out.at[stage], eb.at[stage, g, 1 - dh, (dw + 1) // 2], dh, dw, dt,
+                source((dw + 1) // 2), landing(1 - dh, (dw + 1) // 2), dh, dw, dt,
                 sender, receiver,
             )
             for dh, dw in steps if dw
         ]
 
-    def make_edges(stage, tiles):
+    def make_edges(tiles):
         e = jnp.zeros((ch, nw), F32)
-        for (arr, f, h), tile in tiles:
-            j = arr * 16 + f * 8 + h + 1
+        for (f, h), tile in tiles:
+            j = f * 8 + h + 1
             e = jnp.where(lane == j, tile[:, :1], e)
             e = jnp.where(lane == half + j, tile[:, nw - 1 :], e)
-        e_out[stage] = e.astype(BF)
+        out = []
+        for side in range(2):
+            c = jnp.zeros((fold, nw), F32)
+            for i in range(ch // fold):
+                part = e[i * fold : (i + 1) * fold]
+                shift = (i * 16 - half * side) % nw
+                part = pltpu.roll(part, shift, 1) if shift else part
+                c = jnp.where(small_lane // 16 == i, part, c)
+            out.append(c.astype(BF))
+        return out
 
     up, down, left, right = have(-1, 0), have(1, 0), have(0, -1), have(0, 1)
 
@@ -135,16 +149,20 @@
     row_ok = jnp.where(slot_row == 0, flag(up), jnp.where(slot_row == nh + 1, flag(down), 1))
     edge_ok = (side_ok * row_ok) > 0
 
-    def merged(stage, g):
-        v = [
-            jnp.where(lane < half, eb[stage, g, s, 0].astype(F32), eb[stage, g, s, 1].astype(F32))
-            for s in range(3)
-        ]
-        return jnp.where(
-            slot_row == 0,
-            pltpu.roll(v[0], nw - nh, 1),
-            jnp.where(slot_row == nh + 1, pltpu.roll(v[2], nh, 1), v[1]),
-        )
+    def merged(landing):
+        sides = []
+        for side in range(2):
+            v = [landing(s, side)[...].astype(F32) for s in range(3)]
+            m = jnp.where(
+                small_row == 0,
+                pltpu.roll(v[0], nw - nh, 1),
+                jnp.where(small_row == nh + 1, pltpu.roll(v[2], nh, 1), v[1]),
+            )
+            shifts = [(half * side - i * 16) % nw for i in range(ch // fold)]
+            sides.append(
+                jnp.concatenate([pltpu.roll(m, t, 1) if t else m for t in shifts], axis=0)
+            )
+        return jnp.where(lane < half, sides[0], sides[1])
 
     first_tile, up_tile, down_tile = flag(first) > 0, flag(up) > 0, flag(down) > 0
 
@@ -180,26 +198,38 @@
                         else:
                             acc[f, h + k] += part
 
-    g_in, g_mid, b_in, b_mid = (par[:, i : i + 1] for i in range(4))
+    eye = lax.broadcasted_iota(jnp.int32, (ch, ch), 0) == lax.broadcasted_iota(
+        jnp.int32, (ch, ch), 1
+    )
+    g_in, g_mid, b_in, b_mid = (
+        jnp.sum(jnp.where(eye, p[...], 0.0), axis=1, keepdims=True) for p in (p0, p1, p2, p3)
+    )
 
     own = [(f, h) for f in range(nf) for h in range(nh)]
-    make_edges(0, [((a, f, h), x[a, f, h].astype(F32)) for a in range(4) for f, h in own])
+    for a in range(4):
+        sides = make_edges([((f, h), x[a][f, h].astype(F32)) for f, h in own])
+        for side in range(2):
+            e_out0[side, a] = sides[side]
     pl.semaphore_wait(barrier, 2 * rows_near * cols_near - 1)
 
     def x_rows(a, cb, g, dt, sender=None, receiver=None):
-        return rows_of(x.at[a, :, 0], x.at[a, :, nh - 1], cb, g, dt, sender, receiver)
-
-    e_own = edges_of(0, 0, 0)
-    e_other = edges_of(0, 1, 1)
-    s_cot = x_rows(3, cb_cot, 0, 0)
+        return rows_of(x[a].at[:, 0], x[a].at[:, nh - 1], cb, g, dt, sender, receiver)
+
+    def land(k):
+        return lambda slot, side: eb.at[k, slot, side]
+
+    s_in = x_rows(0, cb_in, 1, 1, first, second)
+    s_in += x_rows(0, cb_in, 0, 0)
+    s_in += x_rows(1, cb_in, 1, 0, first, first)
+    s_in += [transfer(x0, cb_in.at[1, :, 1 : nh + 1], 0, 0, 1, first, second)]
+    s_in += edges_of(lambda side: e_out0.at[side], lambda slot, side: eb0.at[slot, side], 0)
+    s_in += edges_of(lambda side: e_out0.at[side, 0], land(0), 1, first, second)
+    s_cot = edges_of(lambda side: e_out0.at[side, 3], land(5), 1, second, first)
     s_cot += x_rows(3, cb_cot, 1, 1, second, first)
-    s_cot += [transfer(x.at[3], cb_cot.at[1, :, 1 : nh + 1], 0, 0, 1, second, first)]
-    s_in = x_rows(0, cb_in, 0, 0)
-    s_in += x_rows(0, cb_in, 1, 1, first, second)
-    s_in += [transfer(x.at[0], cb_in.at[1, :, 1 : nh + 1], 0, 0, 1, first, second)]
-    s_in += x_rows(1, cb_in, 1, 0, first, first)
+    s_cot += x_rows(3, cb_cot, 0, 0)
+    s_cot += [transfer(x3, cb_cot.at[1, :, 1 : nh + 1], 0, 0, 1, second, first)]
     s_cache = x_rows(2, cb_mid, 1, 0, first, first)
-    stage0 = e_own + e_other + s_cot + s_in + s_cache
+    stage0 = s_in + s_cot + s_cache
     start(stage0)
 
     for fwd, w in ((0, w_in), (1, w_mid)):
@@ -213,39 +243,25 @@
                 wts[2 + fwd, t * ch : (t + 1) * ch, ab * ch : (ab + 1) * ch] = turned[
                     (2 - t) * ch : (3 - t) * ch
                 ].astype(BF)
-
-    arrive(e_own + e_other + s_cot)
-    raw_own, raw_other = merged(0, 0), merged(0, 1)
-    e0 = jnp.where(edge_ok, raw_own, 0.0)
-    e1 = jnp.where(edge_ok, jnp.where(first_tile, raw_other, 0.0), 0.0)
-    for f in range(nf):
-        for hp in range(np_):
-            j = 3 * 16 + f * 8 + hp
-            inner = 1 <= hp <= nh
-            tile = x[3, f, hp - 1] if inner else cb_cot[0, f, hp]
-            put(0, f, hp, tile.astype(F32), e0, j)
-            tile = jnp.where(first_tile, cb_cot[1, f, hp].astype(F32), 0.0)
-            put(0, nf + f, hp, tile, e1, j)
-    convolve(0, 3)
-    for f, h in own:
-        grad[f, h] = acc[f, h]
+    for f, h in own:
+        hid[f, h] = act(x0[f, h].astype(F32), g_in).astype(BF)
 
     arrive(s_in)
-    e_in0 = jnp.where(edge_ok, act(raw_own, g_in), 0.0)
-    e_in1 = jnp.where(
-        edge_ok,
-        jnp.where(first_tile, pltpu.roll(raw_own, nw - 16, 1), act(raw_other, g_in)),
-        0.0,
-    )
+
+    def held(a):
+        return merged(lambda slot, side: eb0.at[slot, side, a])
+
+    e0 = jnp.where(edge_ok, act(held(0), g_in), 0.0)
+    e1 = jnp.where(edge_ok, jnp.where(first_tile, held(1), act(merged(land(0)), g_in)), 0.0)
     for f in range(nf):
         for hp in range(np_):
             j = f * 8 + hp
             inner = 1 <= hp <= nh
-            tile = x[0, f, hp - 1] if inner else cb_in[0, f, hp]
-            put(1, nf + f, hp, act(tile.astype(F32), g_in), e_in0, j)
+            tile = hid[f, hp - 1].astype(F32) if inner else act(cb_in[0, f, hp].astype(F32), g_in)
+            put(1, nf + f, hp, tile, e0, j)
             there = cb_in[1, f, hp].astype(F32)
-            here = x[1, f, hp - 1].astype(F32) if inner else there
-            put(1, f, hp, jnp.where(first_tile, here, act(there, g_in)), e_in1, j)
+            here = x1[f, hp - 1].astype(F32) if inner else there
+            put(1, f, hp, jnp.where(first_tile, here, act(there, g_in)), e1, j)
     convolve(1, 0)
     tiles = []
     for f, h in own:
@@ -253,39 +269,55 @@
         hid[f, h] = hidden
         a = act(hidden.astype(F32), g_mid).astype(BF)
         cb_mid[0, f, h + 1] = a
-        tiles.append(((0, f, h), a.astype(F32)))
-    make_edges(1, tiles)
-
-    def later(stage, cb, sender, receiver):
+        tiles.append(((f, h), a.astype(F32)))
+    sides = make_edges(tiles)
+    for side in range(2):
+        e_out[0, side] = sides[side]
+
+    def later(k, cb, sender, receiver):
         top, bottom = cb.at[0, :, 1], cb.at[0, :, nh]
-        items = edges_of(stage, 0, 0) + rows_of(top, bottom, cb, 0, 0)
-        items += edges_of(stage, 1, 1, sender, receiver)
-        items += rows_of(top, bottom, cb, 1, 1, sender, receiver)
+        items = rows_of(top, bottom, cb, 1, 1, sender, receiver)
+        items += rows_of(top, bottom, cb, 0, 0)
         items += [
             transfer(
                 cb.at[0, :, 1 : nh + 1], cb.at[1, :, 1 : nh + 1], 0, 0, 1, sender, receiver
             )
         ]
+        source = lambda side: e_out.at[k, side]
+        items += edges_of(source, land(1 + 2 * k), 0)
+        items += edges_of(source, land(2 + 2 * k), 1, sender, receiver)
         return items
 
-    stage1 = later(1, cb_mid, first, second)
+    stage1 = later(0, cb_mid, first, second)
     start(stage1)
 
+    arrive(s_cot)
+    e0 = jnp.where(edge_ok, held(3), 0.0)
+    e1 = jnp.where(edge_ok, jnp.where(first_tile, merged(land(5)), 0.0), 0.0)
+    for f in range(nf):
+        for hp in range(np_):
+            j = f * 8 + hp
+            inner = 1 <= hp <= nh
+            tile = x3[f, hp - 1] if inner else cb_cot[0, f, hp]
+            put(0, f, hp, tile.astype(F32), e0, j)
+            tile = jnp.where(first_tile, cb_cot[1, f, hp].astype(F32), 0.0)
+            put(0, nf + f, hp, tile, e1, j)
+    convolve(0, 3)
     tiles = []
     for f, h in own:
-        d = act_back(hid[f, h].astype(F32), g_mid, grad[f, h]).astype(BF)
+        d = act_back(hid[f, h].astype(F32), g_mid, acc[f, h]).astype(BF)
         cb_back[0, f, h + 1] = d
-        tiles.append(((0, f, h), d.astype(F32)))
-    make_edges(2, tiles)
-    stage2 = later(2, cb_back, second, first)
+        tiles.append(((f, h), d.astype(F32)))
+    sides = make_edges(tiles)
+    for side in range(2):
+        e_out[1, side] = sides[side]
+    stage2 = later(1, cb_back, second, first)
     start(stage2)
 
     arrive(s_cache)
     arrive(stage1)
-    e0 = jnp.where(edge_ok, merged(1, 0), 0.0)
-    e1 = jnp.where(
-        edge_ok, jnp.where(first_tile, pltpu.roll(raw_own, nw - 32, 1), merged(1, 1)), 0.0
-    )
+    e0 = jnp.where(edge_ok, merged(land(1)), 0.0)
+    e1 = jnp.where(edge_ok, jnp.where(first_tile, held(2), merged(land(2))), 0.0)
     for f in range(nf):
         for hp in range(np_):
             j = f * 8 + hp
@@ -293,15 +325,17 @@
             put(2, nf + f, hp, cb_mid[0, f, hp].astype(F32), e0, j)
             there = cb_mid[1, f, hp].astype(F32)
             if inner:
-                there = jnp.where(first_tile, x[2, f, hp - 1].astype(F32), there)
+                there = jnp.where(first_tile, x2[f, hp - 1].astype(F32), there)
             put(2, f, hp, there, e1, j)
     convolve(2, 1)
     for f, h in own:
-        dec[f, h] = (x[0, f, h].astype(F32) + acc[f, h] + b_mid).astype(BF)
+        wide[f, pl.ds(h, ch, stride=nh), :] = x0[f, h].astype(F32) + acc[f, h] + b_mid
+    for f in range(nf):
+        dec[f] = wide[f].astype(BF)
 
     arrive(stage2)
-    e0 = jnp.where(edge_ok, merged(2, 0), 0.0)
-    e1 = jnp.where(edge_ok, jnp.where(first_tile, merged(2, 1), 0.0), 0.0)
+    e0 = jnp.where(edge_ok, merged(land(3)), 0.0)
+    e1 = jnp.where(edge_ok, jnp.where(first_tile, merged(land(4)), 0.0), 0.0)
     for f in range(nf):
         for hp in range(np_):
             j = f * 8 + hp
@@ -310,7 +344,9 @@
             put(3, nf + f, hp, tile, e1, j)
     convolve(3, 2)
     for f, h in own:
-        grad[f, h] = x[3, f, h].astype(F32) + act_back(x[0, f, h].astype(F32), g_in, acc[f, h])
+        grad[f, pl.ds(h, ch, stride=nh), :] = x3[f, h].astype(F32) + act_back(
+            x0[f, h].astype(F32), g_in, acc[f, h]
+        )
     leave(stage0 + stage1 + stage2)
 
 
@@ -319,8 +355,8 @@
     bias_mid, cotangent,
 ):
     nf, ch, nh, nw = frames.shape
-    x = jnp.stack([frames, cache_in, cache_mid, cotangent]).transpose(0, 1, 3, 2, 4)
-    par = jnp.stack([gain_in, gain_mid, bias_in, bias_mid], 1)
+    x = [v.transpose(0, 2, 1, 3) for v in (frames, cache_in, cache_mid, cotangent)]
+    rows = [v.reshape(1, ch) for v in (gain_in, gain_mid, bias_in, bias_mid)]
     k = 3 * ch
     vmem = pl.BlockSpec(memory_space=pltpu.VMEM)
     center = pltpu.VMEM((2, nf, nh + 2, ch, nw), BF)
@@ -328,18 +364,21 @@
     dec, grad = pl.pallas_call(
         functools.partial(kernel, lax.axis_size("ha"), lax.axis_size("wa")),
         out_shape=(
-            jax.ShapeDtypeStruct((nf, nh, ch, nw), BF),
-            jax.ShapeDtypeStruct((nf, nh, ch, nw), F32),
+            jax.ShapeDtypeStruct((nf, ch * nh, nw), BF),
+            jax.ShapeDtypeStruct((nf, ch * nh, nw), F32),
         ),
-        in_specs=[vmem] * 4,
+        in_specs=[vmem] * 10,
         out_specs=(vmem, vmem),
         scratch_shapes=[
             center, center, center, center,
-            pltpu.VMEM((3, 2, 3, 2, ch, nw), BF),
-            pltpu.VMEM((3, ch, nw), BF),
+            pltpu.VMEM((3, 2, 4, 16, nw), BF),
+            pltpu.VMEM((6, 3, 2, 16, nw), BF),
+            pltpu.VMEM((2, 4, 16, nw), BF),
+            pltpu.VMEM((2, 2, 16, nw), BF),
             pltpu.VMEM((4, nf + 2, (nh + 2) * k, nw), BF),
             pltpu.VMEM((4, k, 9 * ch), BF),
             pltpu.VMEM((nf, nh, ch, nw), F32),
+            pltpu.VMEM((nf, ch * nh, nw), F32),
             pltpu.VMEM((nf, nh, ch, nw), BF),
             pltpu.SemaphoreType.DMA((copies,)),
             pltpu.SemaphoreType.DMA((copies,)),
@@ -347,8 +386,8 @@
         compiler_params=pltpu.CompilerParams(
             collective_id=0, has_side_effects=True, vmem_limit_bytes=60 << 20
         ),
-    )(x, weight_in.reshape(9, ch, k), weight_mid.reshape(9, ch, k), par)
-    return dec.transpose(0, 2, 1, 3), grad.transpose(0, 2, 1, 3)
+    )(*x, weight_in.reshape(9, ch, k), weight_mid.reshape(9, ch, k), *rows)
+    return dec.reshape(nf, ch, nh, nw), grad.reshape(nf, ch, nh, nw)
 
 
 def solution(mesh):

time: 33.2 us -> 30.8 us (0.928); the launches traced: 32.7 us -> 30.7 us
  other arithmetic: 0.99 us -> 0 us
  Pallas kernels: 25.5 us -> 24.8 us
    transpose x0 -> x2, local copies, waits for them, and re-layouts: none -> 2.69 us  [per_device(): v.transpose(0, 2, 1, 3)]
    another operation x3 -> x0, local copies, waits for them, and re-layouts: 1.91 us -> none  [the longest x2 1.19 us: per_device(): jnp.stack([frames, cache_in, cache_mid, cotangent]).transpose(0, 1, 3, 2, 4)]
    unnamed x16 -> x8, local copies, waits for them, and re-layouts: 3.56 us -> 2.48 us
    transpose x1 -> x0, other arithmetic: 0.98 us -> none  [per_device(): jnp.stack([frames, cache_in, cache_mid, cotangent]).transpose(0, 1, 3, 2, 4)]
    pallas_call x1, Pallas kernels: 25.5 us -> 24.8 us  [per_device(): pl.pallas_call(functools.partial(kernel, lax.axis_size('ha'), lax.axis_si...]
where the time goes in v2:
time: 30.8 us; the launch traced here: 30.7 us
  Pallas kernels  24.8 us (81%)
  local copies, waits for them, and re-layouts  5.17 us (17%)
  between operations  0.67 us (2%)
    pallas_call x1, Pallas kernels, per_device(): pl.pallas_call(functools.partial(kernel, lax.axis_size('ha'), lax.axis_si...  24.8 us
    transpose x2, local copies, waits for them, and re-layouts, per_device(): v.transpose(0, 2, 1, 3)  2.69 us
    unnamed x8, local copies, waits for them, and re-layouts  2.48 us

profile of v2, /device:TPU:0, one launch (start us, length us, event | category | flops | bytes accessed | tf_op | source)
XLA Modules:
  0.0 30.7 jit_solution(15156560366734983815)
XLA Ops:
  0.6 0.0 copy-start.1
  0.6 0.0 copy-start.2
  0.7 1.9 %copy_bitcast_fusion.2 = (bf16[2,4,96,128]{3,2,1,0:T(8,128)(2,1)}, bf16[2,4,96,128]{3,2,1,0:T(8,128)(2,1)}) fusion(bf16[2,96,4,128]{3,2,1,0:T(4,128)(2,1)} %param.11, bf16[2,96,4,128]{3,2,1,0:T(4,128)(2,1)} %param.10), kind=kLoop, calls=%fused_computation.2 | loop fusion | bytes 786432 | tf_op jit(solution)/shard_map/transpose | solution.py:358
  2.5 0.0 copy-done.1
  2.5 0.0 copy-done.2
  2.5 0.8 %copy_bitcast_fusion = (bf16[2,4,96,128]{3,2,1,0:T(8,128)(2,1)}, bf16[2,4,96,128]{3,2,1,0:T(8,128)(2,1)}) fusion(bf16[2,96,4,128]{3,2,1,0:T(4,128)(2,1)S(1)} %copy-done.1, bf16[2,96,4,128]{3,2,1,0:T(4,128)(2,1)S(1)} %copy-done.2), kind=kLoop, calls=%fused_computation | loop fusion | bytes 786432 | tf_op jit(solution)/shard_map/transpose | solution.py:358
  3.3 24.8 %shard_map.113 = (bf16[2,384,128]{2,1,0:T(8,128)(2,1)}, f32[2,384,128]{2,1,0:T(8,128)}) custom-call(bf16[2,4,96,128]{3,2,1,0:T(8,128)(2,1)} %get-tuple-element.9.x0, bf16[2,4,96,128]{3,2,1,0:T(8,128)(2,1)} %get-tuple-element.8.x1, bf16[2,4,96,128]{3,2,1,0:T(8,128)(2,1)} %get-tuple-element.7.x2, bf16[2,4,96,128]{3,2,1,0:T(8,128)(2,1)} %get-tuple-element.6.x3, ...), custom_call_target="tpu_custom_call" | custom-call | tf_op jit(solution)/shard_map/pallas_call | solution.py:364
  28.2 0.0 copy-start
  28.2 1.7 %copy.22 = bf16[2,96,4,128]{3,2,1,0:T(4,128)(2,1)} copy(bf16[2,96,4,128]{3,2,1,0:T(4,128)(2,1)} %bitcast.19) | data formatting | bytes 393216
  29.9 0.0 copy-done
  29.9 0.7 %copy.23 = f32[2,96,4,128]{3,2,1,0:T(4,128)} copy(f32[2,96,4,128]{3,2,1,0:T(4,128)S(1)} %bitcast.18) | data formatting | bytes 786432
Async XLA Ops:
  0.6 1.9 %copy-start.1 = (bf16[2,96,4,128]{3,2,1,0:T(4,128)(2,1)S(1)}, bf16[2,96,4,128]{3,2,1,0:T(4,128)(2,1)}, u32[]{:S(2)}) copy-start(bf16[2,96,4,128]{3,2,1,0:T(4,128)(2,1)} %param.19) | copy-start | bytes 589828
  0.6 1.9 %copy-start.2 = (bf16[2,96,4,128]{3,2,1,0:T(4,128)(2,1)S(1)}, bf16[2,96,4,128]{3,2,1,0:T(4,128)(2,1)}, u32[]{:S(2)}) copy-start(bf16[2,96,4,128]{3,2,1,0:T(4,128)(2,1)} %param.12) | copy-start | bytes 589828
  28.2 1.7 %copy-start = (f32[2,384,128]{2,1,0:T(8,128)S(1)}, f32[2,384,128]{2,1,0:T(8,128)}, u32[]{:S(2)}) copy-start(f32[2,384,128]{2,1,0:T(8,128)} %get-tuple-element.5) | copy-start | bytes 1179652

commit v3 on v2

--- a/solution.py
+++ b/solution.py
@@ -384,7 +384,7 @@
             pltpu.SemaphoreType.DMA((copies,)),
         ],
         compiler_params=pltpu.CompilerParams(
-            collective_id=0, has_side_effects=True, vmem_limit_bytes=60 << 20
+            collective_id=0, has_side_effects=True, vmem_limit_bytes=24 << 20
         ),
     )(*x, weight_in.reshape(9, ch, k), weight_mid.reshape(9, ch, k), *rows)
     return dec.reshape(nf, ch, nh, nw), grad.reshape(nf, ch, nh, nw)

time: 30.8 us -> 27.6 us (0.90)
  Pallas kernels: 24.8 us -> 22.4 us
  local copies, waits for them, and re-layouts: 5.17 us -> 4.26 us
    pallas_call x1, Pallas kernels: 24.8 us -> 22.4 us  [per_device(): pl.pallas_call(functools.partial(kernel, lax.axis_size('ha'), lax.axis_si...]
    transpose x2, local copies, waits for them, and re-layouts: 2.69 us -> 2.18 us  [per_device(): v.transpose(0, 2, 1, 3)]
    unnamed x8 -> x16, local copies, waits for them, and re-layouts: 2.48 us -> 2.08 us
where the time goes in v3:
time: 27.6 us; the launch traced here: 27.4 us
  Pallas kernels  22.4 us (81%)
  local copies, waits for them, and re-layouts  4.26 us (15%)
  between operations  0.74 us (3%)
    pallas_call x1, Pallas kernels, per_device(): pl.pallas_call(functools.partial(kernel, lax.axis_size('ha'), lax.axis_si...  22.4 us
    transpose x2, local copies, waits for them, and re-layouts, per_device(): v.transpose(0, 2, 1, 3)  2.18 us
    unnamed x16, local copies, waits for them, and re-layouts  2.08 us

profile of v3, /device:TPU:0, one launch (start us, length us, event | category | flops | bytes accessed | tf_op | source)
XLA Modules:
  0.0 27.4 jit_solution(1469729651067910038)
XLA Ops:
  0.6 0.0 copy-start.6
  0.6 0.0 copy-start
  0.7 0.0 copy-start.1
  0.7 1.2 %copy_bitcast_fusion.2 = (bf16[2,4,96,128]{3,2,1,0:T(8,128)(2,1)S(1)}, bf16[2,4,96,128]{3,2,1,0:T(8,128)(2,1)S(1)}) fusion(bf16[2,96,4,128]{3,2,1,0:T(4,128)(2,1)} %param.11, bf16[2,96,4,128]{3,2,1,0:T(4,128)(2,1)} %param.10), kind=kLoop, calls=%fused_computation.2 | loop fusion | bytes 786432 | tf_op jit(solution)/shard_map/transpose | solution.py:358
  1.9 0.0 copy-done.6
  1.9 0.0 copy-start.5
  1.9 1.0 %copy_bitcast_fusion = (bf16[2,4,96,128]{3,2,1,0:T(8,128)(2,1)S(1)}, bf16[2,4,96,128]{3,2,1,0:T(8,128)(2,1)S(1)}) fusion(bf16[2,96,4,128]{3,2,1,0:T(4,128)(2,1)S(1)} %copy-done.6, bf16[2,96,4,128]{3,2,1,0:T(4,128)(2,1)} %param.12), kind=kLoop, calls=%fused_computation | loop fusion | bytes 786432 | tf_op jit(solution)/shard_map/transpose | solution.py:358
  2.9 0.0 copy-start.2
  2.9 0.0 copy-start.3
  2.9 0.0 copy-start.4
  2.9 0.0 copy-done
  2.9 0.0 copy-done.1
  2.9 0.0 copy-done.5
  2.9 0.6 %copy-done.2 = f32[96]{0:T(128)S(1)} copy-done((f32[96]{0:T(128)S(1)}, f32[96]{0:T(128)}, u32[]{:S(2)}) %copy-start.2) | copy-done | bytes 408
  3.5 0.0 copy-done.3
  3.6 0.0 copy-done.4
  3.6 22.4 %shard_map.113 = (bf16[2,384,128]{2,1,0:T(8,128)(2,1)S(1)}, f32[2,384,128]{2,1,0:T(8,128)S(1)}) custom-call(bf16[2,4,96,128]{3,2,1,0:T(8,128)(2,1)S(1)} %get-tuple-element.9.x0, bf16[2,4,96,128]{3,2,1,0:T(8,128)(2,1)S(1)} %get-tuple-element.8.x1, bf16[2,4,96,128]{3,2,1,0:T(8,128)(2,1)S(1)} %get-tuple-element.7.x2, ...), custom_call_target="tpu_custom_call" | custom-call | tf_op jit(solution)/shard_map/pallas_call | solution.py:364
  26.0 0.7 %copy.22 = bf16[2,96,4,128]{3,2,1,0:T(4,128)(2,1)} copy(bf16[2,96,4,128]{3,2,1,0:T(4,128)(2,1)S(1)} %bitcast.19) | data formatting | bytes 393216
  26.7 0.7 %copy.23 = f32[2,96,4,128]{3,2,1,0:T(4,128)} copy(f32[2,96,4,128]{3,2,1,0:T(4,128)S(1)} %bitcast.18) | data formatting | bytes 786432
Async XLA Ops:
  0.6 1.2 %copy-start.6 = (bf16[2,96,4,128]{3,2,1,0:T(4,128)(2,1)S(1)}, bf16[2,96,4,128]{3,2,1,0:T(4,128)(2,1)}, u32[]{:S(2)}) copy-start(bf16[2,96,4,128]{3,2,1,0:T(4,128)(2,1)} %param.19) | copy-start | bytes 589828
  0.6 2.3 %copy-start = (bf16[3,3,96,288]{3,2,1,0:T(8,128)(2,1)S(1)}, bf16[3,3,96,288]{3,2,1,0:T(8,128)(2,1)}, u32[]{:S(2)}) copy-start(bf16[3,3,96,288]{3,2,1,0:T(8,128)(2,1)} %param.15) | copy-start | bytes 1492996
  0.7 2.3 %copy-start.1 = (bf16[3,3,96,288]{3,2,1,0:T(8,128)(2,1)S(1)}, bf16[3,3,96,288]{3,2,1,0:T(8,128)(2,1)}, u32[]{:S(2)}) copy-start(bf16[3,3,96,288]{3,2,1,0:T(8,128)(2,1)} %param.17) | copy-start | bytes 1492996
  1.9 1.1 %copy-start.5 = (f32[96]{0:T(128)S(1)}, f32[96]{0:T(128)}, u32[]{:S(2)}) copy-start(f32[96]{0:T(128)} %param.18) | copy-start | bytes 1156
  2.9 0.7 %copy-start.2 = (f32[96]{0:T(128)S(1)}, f32[96]{0:T(128)}, u32[]{:S(2)}) copy-start(f32[96]{0:T(128)} %param.13) | copy-start | bytes 1156
  2.9 0.7 %copy-start.3 = (f32[96]{0:T(128)S(1)}, f32[96]{0:T(128)}, u32[]{:S(2)}) copy-start(f32[96]{0:T(128)} %param.14) | copy-start | bytes 1156
  2.9 0.7 %copy-start.4 = (f32[96]{0:T(128)S(1)}, f32[96]{0:T(128)}, u32[]{:S(2)}) copy-start(f32[96]{0:T(128)} %param.16) | copy-start | bytes 1156
